TPU v7x, 32 devices: a whole 2x2x4 slice. The times are simulated.
32 devices in a mesh: grp: 2 (over x), row: 2 (over core), col: 8 (over z, y).
Axes of the slice: x: 2, y: 2, z: 4, core: 2. Of those that a mesh axis runs over, the one named last changes fastest.
Arguments:
- hidden_acts: bfloat16 [512, 26624], P(('grp', 'row'), 'col'), parts along dimension 0, may hold values from -216 to 216
- down_weight: bfloat16 [26624, 8192], P('col', 'row'), may hold values from -0.0390625 to 0.0390625
- amax_history: float32 [8], P('grp'), parts along dimension 0, may hold values from 3 to 12
Outputs:
- scaled_out: bfloat16 [512, 8192], P(('grp', 'col'), 'row'), parts along dimension 0
- token_scale: float32 [512], P(('grp', 'row')), parts along dimension 0
- history_next: float32 [8], P('grp'), parts along dimension 0
There are 2 independent parts, one for each index of `grp`. A program takes and returns all parts, laid end to end along the dimension named above; an argument that names none is the same for every part. Nothing has to cross between parts.
All inputs are finite; a program needn't handle non-finite values.
Results may differ from a plain program's by a relative error of at most 0.0044.
Values may be sent and summed in bfloat16 or wider, within the bound.
No kernel may reach another device: no remote copies, remote signals or barrier semaphores. Data moves between devices by JAX's collectives and lax.ppermute only.
A program may use at most 64 MiB of HBM per device.

v0:
```python
import jax
import jax.numpy as jnp
from jax import lax
from jax.sharding import PartitionSpec as P

clip_ratio = 0.5
format_limit = 448.0


def clip_scaled(values, scales):
    return jnp.clip(
        values.astype(jnp.float32) / scales[:, None], -format_limit, format_limit
    ).astype(jnp.bfloat16)


def on_device(hidden_acts, down_weight, amax_history):
    local_peak = jnp.max(jnp.abs(hidden_acts), axis=1).astype(jnp.float32)
    token_peak = lax.pmax(local_peak, "col")
    own_scale = clip_ratio * (token_peak + 1e-06) / format_limit
    quantized = clip_scaled(hidden_acts, own_scale)
    all_quant = lax.all_gather(quantized, "row", axis=0, tiled=True)
    all_scale = lax.all_gather(own_scale, "row", axis=0, tiled=True)
    previous = jnp.max(amax_history)
    block_rows = all_quant.shape[0] // lax.axis_size("col")
    summed = lax.psum_scatter(
        jnp.dot(all_quant, down_weight, preferred_element_type=jnp.float32),
        "col",
        scatter_dimension=0,
        tiled=True,
    )
    block_scale = lax.dynamic_slice_in_dim(
        all_scale, lax.axis_index("col") * block_rows, block_rows
    )
    result = summed * block_scale[:, None]
    local_max = jnp.max(jnp.abs(result))
    scaled_out = jnp.clip(result / previous, -1.0, 1.0).astype(jnp.bfloat16)
    newest = lax.pmax(local_max, ("row", "col"))
    history_next = jnp.concatenate([newest[None], amax_history[:-1]])
    return (scaled_out, own_scale, history_next)


def solution(mesh):
    in_specs = (P(("grp", "row"), "col"), P("col", "row"), P("grp"))
    out_specs = (P(("grp", "col"), "row"), P(("grp", "row")), P("grp"))
    return jax.shard_map(
        on_device, mesh=mesh, in_specs=in_specs, out_specs=out_specs, check_vma=False
    )
```

profile of v0, /device:TPU:0, one launch (start us, length us, event | category | flops | bytes accessed | tf_op | source)
XLA Modules:
  0.0 189.5 jit_solution(5066335631180745152)
XLA Ops:
  7.2 0.0 all-gather.3.cloned.1.call-start
  7.2 1.4 abs_reduce_fusion
  8.6 23.2 %pmax.14 = f32[128]{0:T(128)S(1)} all-reduce(bf16[128]{0:T(256)(128)(2,1)S(1)} %abs_reduce_fusion), channel_id=1, replica_groups=mesh['grp'=2,'row'=2,'col'=8] {'col'}, use_global_device_ids=true, to_apply=%region_1.0 | all-reduce | flops 128 | bytes 768 | tf_op jit(solution)/shard_map/pmax | solution.py:18
  31.8 0.0 copy-start
  31.8 2.3 %clamp_convert_fusion = bf16[128,3328]{1,0:T(8,128)(2,1)} fusion(bf16[128,3328]{1,0:T(8,128)(2,1)} %param.3, f32[128]{0:T(128)S(1)} %add_multiply_fusion), kind=kLoop, calls=%fused_computation | loop fusion | flops 1703936 | bytes 1704448 | tf_op jit(solution)/shard_map/convert_element_type | solution.py:13
  34.1 0.0 all-gather.3.cloned.1.call-update
  34.1 0.0 reduce-scatter.2.cloned.1.call-start
  34.2 7.4 %all-gather.3.cloned.1.call-done = bf16[256,3328]{1,0:T(8,128)(2,1)} async-done(((bf16[128,3328]{1,0:T(8,128)(2,1)}), bf16[256,3328]{1,0:T(8,128)(2,1)}) %all-gather.3.cloned.1.call-update) | async-done | bytes 1703952 | tf_op jit(solution)/shard_map/all_gather | solution.py:21
  41.5 14.3 %fusion = f32[256,4096]{1,0:T(8,128)} fusion(bf16[256,3328]{1,0:T(8,128)(2,1)} %all-gather.3.cloned.1.call-done, bf16[3328,4096]{1,0:T(8,128)(2,1)} %param.4), kind=kOutput, calls=%fused_computation.6 | convolution fusion | flops 6979321856 | bytes 33161216 | tf_op jit(solution)/shard_map/dot_general | solution.py:26
  55.8 0.0 copy-done
  55.8 0.0 copy-start.1
  55.8 0.0 reduce-scatter.2.cloned.1.call-update
  55.9 1.8 all-gather
  57.7 0.1 dynamic_slice.3
  57.7 0.0 copy-done.1
  57.7 0.6 reduce_max.28
  58.3 87.1 %reduce-scatter.2.cloned.1.call-done = f32[32,4096]{1,0:T(8,128)} async-done(((f32[256,4096]{1,0:T(8,128)}), f32[32,4096]{1,0:T(8,128)}) %reduce-scatter.2.cloned.1.call-update) | async-done | bytes 524304 | tf_op jit(solution)/shard_map/reduce_scatter | solution.py:25
  145.5 3.2 %abs_reduce_fusion.1 = (f32[]{:T(128)}, bf16[32,4096]{1,0:T(8,128)(2,1)}) fusion(f32[32,4096]{1,0:T(8,128)} %reduce-scatter.2.cloned.1.call-done, f32[32]{0:T(128)S(1)} %dynamic_slice.3, f32[]{:T(128)} %reduce_max.28), kind=kLoop, calls=%fused_computation.2 | loop fusion | flops 786431 | bytes 786568 | tf_op jit(solution)/shard_map/reduce_max | solution.py:35
  148.7 32.8 %pmax.15 = f32[1]{0:T(128)} all-reduce(f32[1]{0:T(128)} %bitcast.2), channel_id=1, replica_groups=mesh['grp'=2,'row'=2,'col'=8] {'row','col'}, use_global_device_ids=true, to_apply=%region_5.6 | all-reduce | flops 1 | bytes 8 | tf_op jit(solution)/shard_map/pmax | solution.py:37
  181.5 1.1 pad_maximum_fusion
  (2 shorter events, 0.0 us)
Async XLA Ops:
  7.2 34.4 %all-gather.3.cloned.1.call-start = ((), (), s32[]{:S(2)}) async-start(), calls=%async_computation.1 | async-start | bytes 2555904 | tf_op jit(solution)/shard_map/all_gather | solution.py:21
  31.8 24.0 %copy-start = (f32[128]{0:T(128)}, f32[128]{0:T(128)S(1)}, u32[]{:S(2)}) copy-start(f32[128]{0:T(128)S(1)} %add_multiply_fusion) | copy-start | bytes 1540
  34.1 111.3 %reduce-scatter.2.cloned.1.call-start = ((), (), s32[]{:S(2)}) async-start(), calls=%async_computation.2 | async-start | bytes 4718592 | tf_op jit(solution)/shard_map/reduce_scatter | solution.py:25
  55.8 1.9 %copy-start.1 = (f32[4]{0:T(128)S(1)}, f32[4]{0:T(128)}, u32[]{:S(2)}) copy-start(f32[4]{0:T(128)} %param.5) | copy-start | bytes 52
Sparse Core Ops, SparseCore 0:
  34.2 7.2 all-gather.2
  56.0 89.4 reduce-scatter.1
where the time goes:
time: 190 us; the launch traced here: 189 us
  waiting for transfers between devices  94.5 us (50%)
  blocking collectives  57.8 us (30%)
  matrix products  14.3 us (8%)
  between operations  14.1 us (7%)
  other arithmetic  8.67 us (5%)
    reduce_scatter x1, waiting for transfers between devices, on_device(): lax.psum_scatter(jnp.dot(all_quant, down_weight, preferred_element_type=j...  87.1 us
    pmax x1, blocking collectives, on_device(): newest = lax.pmax(local_max, ('row', 'col'))  32.8 us
    pmax x1, blocking collectives, on_device(): token_peak = lax.pmax(local_peak, 'col')  23.2 us
    dot_general x1, matrix products, on_device(): jnp.dot(all_quant, down_weight, preferred_element_type=jnp.float32)  14.3 us
    all_gather x1, waiting for transfers between devices, on_device(): all_quant = lax.all_gather(quantized, 'row', axis=0, tiled=True)  7.35 us
  transfers between devices with their start and end apart: 2, of which 2 were waited for; matrix products, arithmetic and copies ran while one was open for 0% of the time, Pallas kernels for 0%

commit v1 on v0

v1 whole, which is shorter than its diff:
```python
import functools

import jax
import jax.numpy as jnp
from jax import lax
from jax.experimental import pallas as pl
from jax.experimental.pallas import tpu as pltpu
from jax.sharding import PartitionSpec as P


clip_ratio = 0.5
format_limit = 448.0
EIGHTHS = (1, 2, 2, 3)
GROUPS = ((0, 1), (2, 3))


def orders_of(bits):
    orders = [list(range(bits)), list(range(bits))]
    if bits > 1:
        orders[1][:2] = [1, 0]
    return orders


def matmul(lhs_ref, weight_ref, keep_ref, send_ref):
    half, width = keep_ref.shape
    tile = min(512, width)

    @pl.loop(0, width // tile)
    def _(step):
        at = pl.ds(pl.multiple_of(step * tile, tile), tile)
        out = jnp.dot(
            lhs_ref[...], weight_ref[:, at], preferred_element_type=jnp.float32
        )
        keep_ref[:, at] = out[:half]
        send_ref[:, at] = out[half:].astype(jnp.bfloat16)


def first_body(
    cols,
    own_hbm,
    other_ref,
    own_scale,
    other_scale,
    weight_hbm,
    lhs_ref,
    keep_ref,
    send_ref,
    next_ref,
    own_ref,
    weight_ref,
    sems,
):
    bits = cols.bit_length() - 1
    orders = orders_of(bits)
    col, row = lax.axis_index("col"), lax.axis_index("row")
    half = cols // 2
    size = lhs_ref.shape[0] // cols
    width, after = weight_ref.shape[1], next_ref.shape[1]
    own_copy = pltpu.make_async_copy(own_hbm, own_ref, sems.at[0])
    own_copy.start()
    now = pltpu.make_async_copy(weight_hbm.at[:, :width], weight_ref, sems.at[1])
    now.start()

    def position(block):
        away = block ^ col
        where = [
            sum(((away >> bit) & 1) << (bits - 1 - j) for j, bit in enumerate(order))
            for order in orders
        ]
        return jnp.where(row == 0, where[0], where[1])

    def quantize(acts_ref, scale_ref, owner):
        @pl.loop(0, half)
        def _(step):
            at = pl.ds(pl.multiple_of(step * size, size), size)
            to = pl.ds(pl.multiple_of(position(owner * half + step) * size, size), size)
            inverse = 1.0 / scale_ref[at, :]
            values = acts_ref[at, :].astype(jnp.float32) * inverse
            lhs_ref[to, :] = jnp.clip(values, -format_limit, format_limit).astype(
                jnp.bfloat16
            )

    quantize(other_ref, other_scale, 1 - row)
    own_copy.wait()
    later = pltpu.make_async_copy(
        weight_hbm.at[:, width : width + after], next_ref, sems.at[2]
    )
    later.start()
    quantize(own_ref, own_scale, row)
    now.wait()
    matmul(lhs_ref, weight_ref, keep_ref, send_ref)
    later.wait()


def middle_body(
    begin, lhs_ref, weight_ref, weight_hbm, keep_ref, send_ref, next_ref, sem
):
    after = next_ref.shape[1]
    later = pltpu.make_async_copy(
        weight_hbm.at[:, begin : begin + after], next_ref, sem
    )
    later.start()
    matmul(lhs_ref, weight_ref, keep_ref, send_ref)
    later.wait()


def last_body(lhs_ref, weight_ref, keep_ref, send_ref):
    matmul(lhs_ref, weight_ref, keep_ref, send_ref)


def finish_body(history, keep_ref, got_ref, scale_ref, out_ref, peak_ref):
    result = (keep_ref[...] + got_ref[...].astype(jnp.float32)) * scale_ref[...]
    previous = history[0]
    for at in range(1, history.shape[0]):
        previous = jnp.maximum(previous, history[at])
    out_ref[...] = jnp.clip(result / previous, -1.0, 1.0).astype(jnp.bfloat16)
    peak_ref[...] = jnp.full(peak_ref.shape, jnp.max(jnp.abs(result)), jnp.float32)


VMEM = pl.BlockSpec(memory_space=pltpu.VMEM)
SMEM = pl.BlockSpec(memory_space=pltpu.SMEM)
HBM = pl.BlockSpec(memory_space=pltpu.HBM)


def products(own, other, own_scale, other_scale, weight, cols):
    rows, depth = own.shape
    total = 2 * rows
    widths = [weight.shape[1] * part // sum(EIGHTHS) for part in EIGHTHS]
    pair = lambda width: (
        jax.ShapeDtypeStruct((total // 2, width), jnp.float32),
        jax.ShapeDtypeStruct((total // 2, width), jnp.bfloat16),
    )
    piece = lambda width: pltpu.VMEM((depth, width), jnp.bfloat16)
    params = pltpu.CompilerParams(vmem_limit_bytes=12 << 20)
    cost = lambda width: pl.CostEstimate(
        flops=2 * total * depth * width,
        bytes_accessed=2 * depth * width,
        transcendentals=0,
    )
    lhs, *first, held = pl.pallas_call(
        functools.partial(first_body, cols),
        out_shape=(
            jax.ShapeDtypeStruct((total, depth), jnp.bfloat16),
            *pair(widths[0]),
            piece(widths[1]),
        ),
        in_specs=[HBM, VMEM, VMEM, VMEM, HBM],
        out_specs=(VMEM,) * 4,
        scratch_shapes=[
            pltpu.VMEM((rows, depth), jnp.bfloat16),
            pltpu.VMEM((depth, widths[0]), jnp.bfloat16),
            pltpu.SemaphoreType.DMA((3,)),
        ],
        compiler_params=params,
        cost_estimate=cost(widths[0]),
        name="first",
    )(own, other, own_scale, other_scale, weight)
    made = [first]
    begin = widths[0]
    for at in range(1, len(widths)):
        begin += widths[at]
        if at + 1 < len(widths):
            *part, held = pl.pallas_call(
                functools.partial(middle_body, begin),
                out_shape=(*pair(widths[at]), piece(widths[at + 1])),
                in_specs=[VMEM, VMEM, HBM],
                out_specs=(VMEM,) * 3,
                scratch_shapes=[pltpu.SemaphoreType.DMA],
                compiler_params=params,
                cost_estimate=cost(widths[at]),
                name="middle",
            )(lhs, held, weight)
        else:
            part = pl.pallas_call(
                last_body,
                out_shape=pair(widths[at]),
                in_specs=[VMEM, VMEM],
                out_specs=(VMEM,) * 2,
                compiler_params=params,
                cost_estimate=cost(widths[at]),
                name="last",
            )(lhs, held)
        made.append(part)
    return made


def finish(keep, got, scale, history):
    return pl.pallas_call(
        finish_body,
        out_shape=(
            jax.ShapeDtypeStruct(keep.shape, jnp.bfloat16),
            jax.ShapeDtypeStruct((8, 128), jnp.float32),
        ),
        in_specs=[SMEM, VMEM, VMEM, VMEM],
        out_specs=(VMEM, VMEM),
        compiler_params=pltpu.CompilerParams(vmem_limit_bytes=8 << 20),
        cost_estimate=pl.CostEstimate(
            flops=6 * keep.size, bytes_accessed=6 * keep.size, transcendentals=0
        ),
        name="finish",
    )(history, keep, got, scale)


def on_device(hidden_acts, down_weight, amax_history):
    cols = lax.axis_size("col")
    bits = cols.bit_length() - 1
    orders = orders_of(bits)
    col, row = lax.axis_index("col"), lax.axis_index("row")
    block = 2 * hidden_acts.shape[0] // cols

    def across(value, flips):
        pairs = []
        for r in range(2):
            for c in range(cols):
                dr, dc = flips[r]
                pairs.append((r * cols + c, (r ^ dr) * cols + (c ^ dc)))
        return lax.ppermute(value, ("row", "col"), pairs)

    def both(dr, dc):
        return ((dr, dc), (dr, dc))

    def stage(value, at):
        return across(value, tuple((0, 1 << orders[r][at]) for r in range(2)))

    other_acts = across(hidden_acts, both(1, 0))
    peak = jnp.max(jnp.abs(hidden_acts), axis=1).astype(jnp.float32)
    for bit in range(bits):
        peak = jnp.maximum(peak, across(peak, both(0, 1 << bit)))
    own_scale = clip_ratio * (peak + 1e-06) / format_limit
    other_scale = across(own_scale, both(1, 0))

    made = products(
        hidden_acts, other_acts, own_scale[:, None], other_scale[:, None], down_weight, cols
    )
    totals = []
    for keep, send in made:
        got = stage(send, 0)
        totals.append(keep + got.astype(jnp.float32))

    mine = lax.dynamic_slice_in_dim(
        jnp.where(
            row == 0,
            jnp.concatenate([own_scale, other_scale]),
            jnp.concatenate([other_scale, own_scale]),
        ),
        col * block,
        block,
    )[:, None]
    outs, peaks = [], []
    for group in GROUPS:
        total = jnp.concatenate([totals[at] for at in group], axis=1)
        for at in range(1, bits):
            middle = total.shape[0] // 2
            got = stage(total[middle:].astype(jnp.bfloat16), at)
            keep = total[:middle]
            if at < bits - 1:
                total = keep + got.astype(jnp.float32)
        out, top = finish(keep, got, mine, amax_history)
        outs.append(out)
        peaks.append(top)

    newest = functools.reduce(jnp.maximum, peaks)
    flips = [(1, 0)] + [(0, 1 << bit) for bit in range(bits)]
    for at in range(0, len(flips), 2):
        (ar, ac), *more = flips[at : at + 2]
        near = [(ar, ac)]
        for br, bc in more:
            near += [(br, bc), (ar ^ br, ac ^ bc)]
        newest = functools.reduce(
            jnp.maximum, [newest] + [across(newest, both(*flip)) for flip in near]
        )
    history_next = jnp.concatenate([newest[0, :1], amax_history[:-1]])
    return (jnp.concatenate(outs, axis=1), own_scale, history_next)


def solution(mesh):
    in_specs = (P(("grp", "row"), "col"), P("col", "row"), P("grp"))
    out_specs = (P(("grp", "col"), "row"), P(("grp", "row")), P("grp"))
    return jax.shard_map(
        on_device, mesh=mesh, in_specs=in_specs, out_specs=out_specs, check_vma=False
    )
```

time: 190 us -> 94.8 us (0.50)
  waiting for transfers between devices: 94.5 us -> 26.4 us
  blocking collectives: 57.8 us -> 0 us
  starting transfers between devices: 0.08 us -> 28.6 us
  local copies, waits for them, and re-layouts: 0.08 us -> 19.7 us
  Pallas kernels: 0 us -> 15.2 us
  matrix products: 14.3 us -> 0 us
  between operations: 14.1 us -> 0.85 us
  other arithmetic: 8.67 us -> 3.76 us
    reduce_scatter x1 -> x0, waiting for transfers between devices: 87.1 us -> none  [on_device(): lax.psum_scatter(jnp.dot(all_quant, down_weight, preferred_element_type=j...]
    pmax x2 -> x0, blocking collectives: 56 us -> none  [the longest x1 32.8 us: on_device(): newest = lax.pmax(local_max, ('row', 'col'))]
    ppermute x0 -> x19, starting transfers between devices: none -> 28.6 us  [across(): return lax.ppermute(value, ('row', 'col'), pairs)]
    ppermute x0 -> x19, waiting for transfers between devices: none -> 26.4 us  [across(): return lax.ppermute(value, ('row', 'col'), pairs)]
    unnamed x4 -> x10, local copies, waits for them, and re-layouts: 0.01 us -> 18.7 us
    pallas_call x0 -> x6, Pallas kernels: none -> 15.2 us  [the longest x2 6.95 us: products(): pl.pallas_call(functools.partial(middle_body, begin), out_shape=(*pair(wi...]
    dot_general x1 -> x0, matrix products: 14.3 us -> none  [on_device(): jnp.dot(all_quant, down_weight, preferred_element_type=jnp.float32)]
    all_gather x1 -> x0, waiting for transfers between devices: 7.35 us -> none  [on_device(): all_quant = lax.all_gather(quantized, 'row', axis=0, tiled=True)]
  transfers between devices with their start and end apart: 2 -> 19, of which waited for: 2 -> 12; matrix products, arithmetic and copies ran while one was open for 0% -> 3% of each run, Pallas kernels for 0% -> 11%
where the time goes in v1:
time: 94.8 us; the launch traced here: 94.5 us
  starting transfers between devices  28.6 us (30%)
  waiting for transfers between devices  26.4 us (28%)
  local copies, waits for them, and re-layouts  19.7 us (21%)
  Pallas kernels  15.2 us (16%)
  other arithmetic  3.76 us (4%)
    ppermute x19, starting transfers between devices, across(): return lax.ppermute(value, ('row', 'col'), pairs)  28.6 us
    ppermute x19, waiting for transfers between devices, across(): return lax.ppermute(value, ('row', 'col'), pairs)  26.4 us
    unnamed x10, local copies, waits for them, and re-layouts  18.7 us
    pallas_call x2, Pallas kernels, products(): pl.pallas_call(functools.partial(middle_body, begin), out_shape=(*pair(wi...  6.95 us
    pallas_call x1, Pallas kernels, products(): pl.pallas_call(functools.partial(first_body, cols), out_shape=(jax.ShapeD...  3.58 us
    pallas_call x1, Pallas kernels, products(): pl.pallas_call(last_body, out_shape=pair(widths[at]), in_specs=[VMEM, VME...  3.13 us
  transfers between devices with their start and end apart: 19, of which 12 were waited for; matrix products, arithmetic and copies ran while one was open for 3% of the time, Pallas kernels for 11%

profile of v1, /device:TPU:0, one launch (start us, length us, event | category | flops | bytes accessed | tf_op | source)
XLA Modules:
  0.0 94.5 jit_solution(13473682425329932553)
XLA Ops:
  1.2 1.4 %abs_reduce_fusion = bf16[128]{0:T(256)(128)(2,1)S(1)} fusion(bf16[128,3328]{1,0:T(8,128)(2,1)} %own_hbm.1), kind=kLoop, calls=%fused_computation.2 | loop fusion | flops 851840 | bytes 852224 | tf_op jit(solution)/shard_map/reduce_max | solution.py:226
  2.6 2.6 %collective-permute-start.1 = (f32[128]{0:T(128)S(1)}, f32[128]{0:T(128)S(1)}, u32[]{:S(2)}, u32[]{:S(2)}) collective-permute-start(f32[128]{0:T(128)S(1)} %convert_element_type.25), channel_id=1, source_target_pairs={{0,1},{1,0},{2,3},{3,2},{4,5},{5,4},{6,7},{7,6},{8,9},{9,8},{10,11... | collective-permute-start | bytes 1544 | tf_op jit(solution)/shard_map/ppermute | solution.py:217
  5.2 1.5 %collective-permute-done.1 = f32[128]{0:T(128)S(1)} collective-permute-done((f32[128]{0:T(128)S(1)}, f32[128]{0:T(128)S(1)}, u32[]{:S(2)}, u32[]{:S(2)}) %collective-permute-start.1) | collective-permute-done | bytes 544 | tf_op jit(solution)/shard_map/ppermute | solution.py:217
  6.7 2.1 %collective-permute-start.2 = (f32[128]{0:T(128)S(1)}, f32[128]{0:T(128)S(1)}, u32[]{:S(2)}, u32[]{:S(2)}) collective-permute-start(f32[128]{0:T(128)S(1)} %convert_maximum_fusion), channel_id=1, source_target_pairs={{0,2},{1,3},{2,0},{3,1},{4,6},{5,7},{6,4},{7,5},{8,10},{9,11},{10,... | collective-permute-start | bytes 1544 | tf_op jit(solution)/shard_map/ppermute | solution.py:217
  8.8 1.5 %collective-permute-done.2 = f32[128]{0:T(128)S(1)} collective-permute-done((f32[128]{0:T(128)S(1)}, f32[128]{0:T(128)S(1)}, u32[]{:S(2)}, u32[]{:S(2)}) %collective-permute-start.2) | collective-permute-done | bytes 544 | tf_op jit(solution)/shard_map/ppermute | solution.py:217
  10.3 3.0 %collective-permute-start.3 = (f32[128]{0:T(128)S(1)}, f32[128]{0:T(128)S(1)}, u32[]{:S(2)}, u32[]{:S(2)}) collective-permute-start(f32[128]{0:T(128)S(1)} %max.31), channel_id=1, source_target_pairs={{0,4},{1,5},{2,6},{3,7},{4,0},{5,1},{6,2},{7,3},{8,12},{9,13},{10,... | collective-permute-start | bytes 1544 | tf_op jit(solution)/shard_map/ppermute | solution.py:217
  13.4 1.5 %collective-permute-done.3 = f32[128]{0:T(128)S(1)} collective-permute-done((f32[128]{0:T(128)S(1)}, f32[128]{0:T(128)S(1)}, u32[]{:S(2)}, u32[]{:S(2)}) %collective-permute-start.3) | collective-permute-done | bytes 544 | tf_op jit(solution)/shard_map/ppermute | solution.py:217
  16.2 8.7 %copy-done = bf16[3328,4096]{1,0:T(8,128)(2,1)S(1)} copy-done((bf16[3328,4096]{1,0:T(8,128)(2,1)S(1)}, bf16[3328,4096]{1,0:T(8,128)(2,1)}, u32[]{:S(2)}) %copy-start) | copy-done | bytes 27263000
  26.1 3.6 %first.1 = (bf16[256,3328]{1,0:T(8,128)(2,1)S(1)}, f32[128,512]{1,0:T(8,128)S(1)}, bf16[128,512]{1,0:T(8,128)(2,1)S(1)}, bf16[3328,1024]{1,0:T(8,128)(2,1)S(1)}) custom-call(bf16[128,3328]{1,0:T(8,128)(2,1)S(1)} %copy-done.2, bf16[128,3328]{1,0:T(8,128)(2,1)S(1)} %collective-permute-done.other_ref, f32[128,1]{1,0:T(8,128)S(1)} %copy.6.own_scale, ...), custom_call_target="tpu_custom_call" | custom-call | flops 872415232 | bytes 3407872 | tf_op jit(solution)/shard_map/first/pallas_call | solution.py:140
  29.7 1.9 %collective-permute-start.5 = (bf16[128,512]{1,0:T(8,128)(2,1)S(1)}, bf16[128,512]{1,0:T(8,128)(2,1)S(1)}, u32[]{:S(2)}, u32[]{:S(2)}) collective-permute-start(bf16[128,512]{1,0:T(8,128)(2,1)S(1)} %get-tuple-element.20), channel_id=1, source_target_pairs={{0,1},{1,0},{2,3},{3,2},{4,5},{5,4},{6,7},{7,6},{8,10},{9,11},{10,... | collective-permute-start | bytes 393224 | tf_op jit(solution)/shard_map/ppermute | solution.py:217
  31.7 8.8 %copy-done.1 = bf16[3328,4096]{1,0:T(8,128)(2,1)S(1)} copy-done((bf16[3328,4096]{1,0:T(8,128)(2,1)S(1)}, bf16[3328,4096]{1,0:T(8,128)(2,1)}, u32[]{:S(2)}) %copy-start.1) | copy-done | bytes 27263000
  40.4 3.0 %middle.2 = (f32[128,1024]{1,0:T(8,128)S(1)}, bf16[128,1024]{1,0:T(8,128)(2,1)S(1)}, bf16[3328,1024]{1,0:T(8,128)(2,1)S(1)}) custom-call(bf16[256,3328]{1,0:T(8,128)(2,1)S(1)} %get-tuple-element.21.lhs_ref, bf16[3328,1024]{1,0:T(8,128)(2,1)S(1)} %get-tuple-element.22.weight_ref, bf16[3328,4096]{1,0:T(8,128)(2,1)S(1)} %copy-done.1), custom_call_target="tpu_custom_call" | custom-call | flops 1744830464 | bytes 6815744 | tf_op jit(solution)/shard_map/middle/pallas_call | solution.py:163
  43.7 3.9 %middle.3 = (f32[128,1024]{1,0:T(8,128)S(1)}, bf16[128,1024]{1,0:T(8,128)(2,1)S(1)}, bf16[3328,1536]{1,0:T(8,128)(2,1)S(1)}) custom-call(bf16[256,3328]{1,0:T(8,128)(2,1)S(1)} %get-tuple-element.21.lhs_ref, bf16[3328,1024]{1,0:T(8,128)(2,1)S(1)} %get-tuple-element.26.weight_ref, bf16[3328,4096]{1,0:T(8,128)(2,1)} %weight_hbm.5), custom_call_target="tpu_custom_call" | custom-call | flops 1744830464 | bytes 6815744 | tf_op jit(solution)/shard_map/middle/pallas_call | solution.py:163
  47.6 1.9 %collective-permute-start.9 = (bf16[128,1024]{1,0:T(8,128)(2,1)S(1)}, bf16[128,1024]{1,0:T(8,128)(2,1)S(1)}, u32[]{:S(2)}, u32[]{:S(2)}) collective-permute-start(bf16[128,1024]{1,0:T(8,128)(2,1)S(1)} %get-tuple-element.28), channel_id=1, source_target_pairs={{0,1},{1,0},{2,3},{3,2},{4,5},{5,4},{6,7},{7,6},{8,10},{9,11},{10,... | collective-permute-start | bytes 786440 | tf_op jit(solution)/shard_map/ppermute | solution.py:217
  49.5 3.1 %last.1 = (f32[128,1536]{1,0:T(8,128)S(1)}, bf16[128,1536]{1,0:T(8,128)(2,1)S(1)}) custom-call(bf16[256,3328]{1,0:T(8,128)(2,1)S(1)} %get-tuple-element.21.lhs_ref, bf16[3328,1536]{1,0:T(8,128)(2,1)S(1)} %get-tuple-element.29.weight_ref), custom_call_target="tpu_custom_call" | custom-call | flops 2617245696 | bytes 10223616 | tf_op jit(solution)/shard_map/last/pallas_call | solution.py:174
  54.1 6.4 %collective-permute-done.10 = bf16[128,1536]{1,0:T(8,128)(2,1)S(1)} collective-permute-done((bf16[128,1536]{1,0:T(8,128)(2,1)S(1)}, bf16[128,1536]{1,0:T(8,128)(2,1)S(1)}, u32[]{:S(2)}, u32[]{:S(2)}) %collective-permute-start.10) | collective-permute-done | bytes 393248 | tf_op jit(solution)/shard_map/ppermute | solution.py:217
  60.6 1.6 %collective-permute-start.11 = (bf16[64,2560]{1,0:T(8,128)(2,1)S(1)}, bf16[64,2560]{1,0:T(8,128)(2,1)S(1)}, u32[]{:S(2)}, u32[]{:S(2)}) collective-permute-start(bf16[64,2560]{1,0:T(8,128)(2,1)S(1)} %fusion.2), channel_id=1, source_target_pairs={{0,2},{1,3},{2,0},{3,1},{4,6},{5,7},{6,4},{7,5},{8,9},{9,8},{10,11... | collective-permute-start | bytes 983048 | tf_op jit(solution)/shard_map/ppermute | solution.py:217
  62.9 4.9 %collective-permute-done.11 = bf16[64,2560]{1,0:T(8,128)(2,1)S(1)} collective-permute-done((bf16[64,2560]{1,0:T(8,128)(2,1)S(1)}, bf16[64,2560]{1,0:T(8,128)(2,1)S(1)}, u32[]{:S(2)}, u32[]{:S(2)}) %collective-permute-start.11) | collective-permute-done | bytes 327712 | tf_op jit(solution)/shard_map/ppermute | solution.py:217
  67.9 3.8 %collective-permute-start.12 = (bf16[32,2560]{1,0:T(8,128)(2,1)S(1)}, bf16[32,2560]{1,0:T(8,128)(2,1)S(1)}, u32[]{:S(2)}, u32[]{:S(2)}) collective-permute-start(bf16[32,2560]{1,0:T(8,128)(2,1)S(1)} %slice.70), channel_id=1, source_target_pairs={{0,4},{1,5},{2,6},{3,7},{4,0},{5,1},{6,2},{7,3},{8,12},{9,13},{10,... | collective-permute-start | bytes 491528 | tf_op jit(solution)/shard_map/ppermute | solution.py:217
  71.8 3.7 %collective-permute-start.8 = (bf16[32,1536]{1,0:T(8,128)(2,1)S(1)}, bf16[32,1536]{1,0:T(8,128)(2,1)S(1)}, u32[]{:S(2)}, u32[]{:S(2)}) collective-permute-start(bf16[32,1536]{1,0:T(8,128)(2,1)S(1)} %slice.71), channel_id=1, source_target_pairs={{0,4},{1,5},{2,6},{3,7},{4,0},{5,1},{6,2},{7,3},{8,12},{9,13},{10,... | collective-permute-start | bytes 294920 | tf_op jit(solution)/shard_map/ppermute | solution.py:217
  75.6 4.5 %collective-permute-done.8.got_ref = bf16[32,1536]{1,0:T(8,128)(2,1)S(1)} collective-permute-done((bf16[32,1536]{1,0:T(8,128)(2,1)S(1)}, bf16[32,1536]{1,0:T(8,128)(2,1)S(1)}, u32[]{:S(2)}, u32[]{:S(2)}) %collective-permute-start.8) | collective-permute-done | bytes 98336 | tf_op jit(solution)/shard_map/ppermute | solution.py:217
  85.8 2.3 %collective-permute-start.18 = (f32[8,128]{1,0:T(8,128)S(1)}, f32[8,128]{1,0:T(8,128)S(1)}, u32[]{:S(2)}, u32[]{:S(2)}) collective-permute-start(f32[8,128]{1,0:T(8,128)S(1)} %maximum_maximum_fusion.1), channel_id=1, source_target_pairs={{0,6},{1,7},{2,4},{3,5},{4,2},{5,3},{6,0},{7,1},{8,14},{9,15},{10,... | collective-permute-start | bytes 12296 | tf_op jit(solution)/shard_map/ppermute | solution.py:217
  88.2 2.1 %collective-permute-start.16 = (f32[8,128]{1,0:T(8,128)S(1)}, f32[8,128]{1,0:T(8,128)S(1)}, u32[]{:S(2)}, u32[]{:S(2)}) collective-permute-start(f32[8,128]{1,0:T(8,128)S(1)} %maximum_maximum_fusion.1), channel_id=1, source_target_pairs={{0,2},{1,3},{2,0},{3,1},{4,6},{5,7},{6,4},{7,5},{8,10},{9,11},{10,... | collective-permute-start | bytes 12296 | tf_op jit(solution)/shard_map/ppermute | solution.py:217
  91.3 1.4 %collective-permute-done.17 = f32[8,128]{1,0:T(8,128)S(1)} collective-permute-done((f32[8,128]{1,0:T(8,128)S(1)}, f32[8,128]{1,0:T(8,128)S(1)}, u32[]{:S(2)}, u32[]{:S(2)}) %collective-permute-start.17) | collective-permute-done | bytes 4128 | tf_op jit(solution)/shard_map/ppermute | solution.py:217
  (58 shorter events, 14.2 us)
Async XLA Ops:
  0.6 15.6 %collective-permute-start = (bf16[128,3328]{1,0:T(8,128)(2,1)}, bf16[128,3328]{1,0:T(8,128)(2,1)S(1)}, u32[]{:S(2)}, u32[]{:S(2)}) collective-permute-start(bf16[128,3328]{1,0:T(8,128)(2,1)} %own_hbm.1), channel_id=1, source_target_pairs={{0,8},{1,9},{2,10},{3,11},{4,12},{5,13},{6,14},{7,15},{8,0},{9,1},... | collective-permute-start | bytes 2555912 | tf_op jit(solution)/shard_map/ppermute | solution.py:217
  2.6 4.1 %collective-permute-start.1 = (f32[128]{0:T(128)S(1)}, f32[128]{0:T(128)S(1)}, u32[]{:S(2)}, u32[]{:S(2)}) collective-permute-start(f32[128]{0:T(128)S(1)} %convert_element_type.25), channel_id=1, source_target_pairs={{0,1},{1,0},{2,3},{3,2},{4,5},{5,4},{6,7},{7,6},{8,9},{9,8},{10,11... | collective-permute-start | bytes 1544 | tf_op jit(solution)/shard_map/ppermute | solution.py:217
  6.7 3.6 %collective-permute-start.2 = (f32[128]{0:T(128)S(1)}, f32[128]{0:T(128)S(1)}, u32[]{:S(2)}, u32[]{:S(2)}) collective-permute-start(f32[128]{0:T(128)S(1)} %convert_maximum_fusion), channel_id=1, source_target_pairs={{0,2},{1,3},{2,0},{3,1},{4,6},{5,7},{6,4},{7,5},{8,10},{9,11},{10,... | collective-permute-start | bytes 1544 | tf_op jit(solution)/shard_map/ppermute | solution.py:217
  10.3 4.6 %collective-permute-start.3 = (f32[128]{0:T(128)S(1)}, f32[128]{0:T(128)S(1)}, u32[]{:S(2)}, u32[]{:S(2)}) collective-permute-start(f32[128]{0:T(128)S(1)} %max.31), channel_id=1, source_target_pairs={{0,4},{1,5},{2,6},{3,7},{4,0},{5,1},{6,2},{7,3},{8,12},{9,13},{10,... | collective-permute-start | bytes 1544 | tf_op jit(solution)/shard_map/ppermute | solution.py:217
  14.9 14.8 %copy-start.4 = (f32[128]{0:T(128)}, f32[128]{0:T(128)S(1)}, u32[]{:S(2)}) copy-start(f32[128]{0:T(128)S(1)} %add_multiply_fusion) | copy-start | bytes 1540
  14.9 1.2 %collective-permute-start.4 = (f32[128]{0:T(128)S(1)}, f32[128]{0:T(128)S(1)}, u32[]{:S(2)}, u32[]{:S(2)}) collective-permute-start(f32[128]{0:T(128)S(1)} %add_multiply_fusion), channel_id=1, source_target_pairs={{0,8},{1,9},{2,10},{3,11},{4,12},{5,13},{6,14},{7,15},{8,0},{9,1},... | collective-permute-start | bytes 1544 | tf_op jit(solution)/shard_map/ppermute | solution.py:217
  16.2 8.8 %copy-start = (bf16[3328,4096]{1,0:T(8,128)(2,1)S(1)}, bf16[3328,4096]{1,0:T(8,128)(2,1)}, u32[]{:S(2)}) copy-start(bf16[3328,4096]{1,0:T(8,128)(2,1)} %weight_hbm.5) | copy-start | bytes 81788928
  25.0 1.2 %copy-start.2 = (bf16[128,3328]{1,0:T(8,128)(2,1)S(1)}, bf16[128,3328]{1,0:T(8,128)(2,1)}, u32[]{:S(2)}) copy-start(bf16[128,3328]{1,0:T(8,128)(2,1)} %own_hbm.1) | copy-start | bytes 2555908
  29.7 23.2 %collective-permute-start.5 = (bf16[128,512]{1,0:T(8,128)(2,1)S(1)}, bf16[128,512]{1,0:T(8,128)(2,1)S(1)}, u32[]{:S(2)}, u32[]{:S(2)}) collective-permute-start(bf16[128,512]{1,0:T(8,128)(2,1)S(1)} %get-tuple-element.20), channel_id=1, source_target_pairs={{0,1},{1,0},{2,3},{3,2},{4,5},{5,4},{6,7},{7,6},{8,10},{9,11},{10,... | collective-permute-start | bytes 393224 | tf_op jit(solution)/shard_map/ppermute | solution.py:217
  31.7 8.8 %copy-start.1 = (bf16[3328,4096]{1,0:T(8,128)(2,1)S(1)}, bf16[3328,4096]{1,0:T(8,128)(2,1)}, u32[]{:S(2)}) copy-start(bf16[3328,4096]{1,0:T(8,128)(2,1)} %weight_hbm.5) | copy-start | bytes 81788928
  43.5 18.8 %collective-permute-start.6 = (bf16[128,1024]{1,0:T(8,128)(2,1)S(1)}, bf16[128,1024]{1,0:T(8,128)(2,1)S(1)}, u32[]{:S(2)}, u32[]{:S(2)}) collective-permute-start(bf16[128,1024]{1,0:T(8,128)(2,1)S(1)} %get-tuple-element.24), channel_id=1, source_target_pairs={{0,1},{1,0},{2,3},{3,2},{4,5},{5,4},{6,7},{7,6},{8,10},{9,11},{10,... | collective-permute-start | bytes 786440 | tf_op jit(solution)/shard_map/ppermute | solution.py:217
  47.6 6.4 %collective-permute-start.9 = (bf16[128,1024]{1,0:T(8,128)(2,1)S(1)}, bf16[128,1024]{1,0:T(8,128)(2,1)S(1)}, u32[]{:S(2)}, u32[]{:S(2)}) collective-permute-start(bf16[128,1024]{1,0:T(8,128)(2,1)S(1)} %get-tuple-element.28), channel_id=1, source_target_pairs={{0,1},{1,0},{2,3},{3,2},{4,5},{5,4},{6,7},{7,6},{8,10},{9,11},{10,... | collective-permute-start | bytes 786440 | tf_op jit(solution)/shard_map/ppermute | solution.py:217
  52.7 27.5 %copy-start.3 = (f32[4]{0:T(128)S(1)}, f32[4]{0:T(128)}, u32[]{:S(2)}) copy-start(f32[4]{0:T(128)} %history.3) | copy-start | bytes 52
  52.7 7.8 %collective-permute-start.10 = (bf16[128,1536]{1,0:T(8,128)(2,1)S(1)}, bf16[128,1536]{1,0:T(8,128)(2,1)S(1)}, u32[]{:S(2)}, u32[]{:S(2)}) collective-permute-start(bf16[128,1536]{1,0:T(8,128)(2,1)S(1)} %get-tuple-element.31), channel_id=1, source_target_pairs={{0,1},{1,0},{2,3},{3,2},{4,5},{5,4},{6,7},{7,6},{8,10},{9,11},{10,... | collective-permute-start | bytes 1179656 | tf_op jit(solution)/shard_map/ppermute | solution.py:217
  60.6 7.1 %collective-permute-start.11 = (bf16[64,2560]{1,0:T(8,128)(2,1)S(1)}, bf16[64,2560]{1,0:T(8,128)(2,1)S(1)}, u32[]{:S(2)}, u32[]{:S(2)}) collective-permute-start(bf16[64,2560]{1,0:T(8,128)(2,1)S(1)} %fusion.2), channel_id=1, source_target_pairs={{0,2},{1,3},{2,0},{3,1},{4,6},{5,7},{6,4},{7,5},{8,9},{9,8},{10,11... | collective-permute-start | bytes 983048 | tf_op jit(solution)/shard_map/ppermute | solution.py:217
  62.4 9.3 %collective-permute-start.7 = (bf16[64,1536]{1,0:T(8,128)(2,1)S(1)}, bf16[64,1536]{1,0:T(8,128)(2,1)S(1)}, u32[]{:S(2)}, u32[]{:S(2)}) collective-permute-start(bf16[64,1536]{1,0:T(8,128)(2,1)S(1)} %fusion.5), channel_id=1, source_target_pairs={{0,2},{1,3},{2,0},{3,1},{4,6},{5,7},{6,4},{7,5},{8,9},{9,8},{10,11... | collective-permute-start | bytes 589832 | tf_op jit(solution)/shard_map/ppermute | solution.py:217
  67.9 13.0 %collective-permute-start.12 = (bf16[32,2560]{1,0:T(8,128)(2,1)S(1)}, bf16[32,2560]{1,0:T(8,128)(2,1)S(1)}, u32[]{:S(2)}, u32[]{:S(2)}) collective-permute-start(bf16[32,2560]{1,0:T(8,128)(2,1)S(1)} %slice.70), channel_id=1, source_target_pairs={{0,4},{1,5},{2,6},{3,7},{4,0},{5,1},{6,2},{7,3},{8,12},{9,13},{10,... | collective-permute-start | bytes 491528 | tf_op jit(solution)/shard_map/ppermute | solution.py:217
  71.8 8.4 %collective-permute-start.8 = (bf16[32,1536]{1,0:T(8,128)(2,1)S(1)}, bf16[32,1536]{1,0:T(8,128)(2,1)S(1)}, u32[]{:S(2)}, u32[]{:S(2)}) collective-permute-start(bf16[32,1536]{1,0:T(8,128)(2,1)S(1)} %slice.71), channel_id=1, source_target_pairs={{0,4},{1,5},{2,6},{3,7},{4,0},{5,1},{6,2},{7,3},{8,12},{9,13},{10,... | collective-permute-start | bytes 294920 | tf_op jit(solution)/shard_map/ppermute | solution.py:217
  81.7 3.1 %collective-permute-start.15 = (f32[8,128]{1,0:T(8,128)S(1)}, f32[8,128]{1,0:T(8,128)S(1)}, u32[]{:S(2)}, u32[]{:S(2)}) collective-permute-start(f32[8,128]{1,0:T(8,128)S(1)} %max.33), channel_id=1, source_target_pairs={{0,9},{1,8},{2,11},{3,10},{4,13},{5,12},{6,15},{7,14},{8,1},{9,0},... | collective-permute-start | bytes 12296 | tf_op jit(solution)/shard_map/ppermute | solution.py:217
  82.2 3.6 %collective-permute-start.14 = (f32[8,128]{1,0:T(8,128)S(1)}, f32[8,128]{1,0:T(8,128)S(1)}, u32[]{:S(2)}, u32[]{:S(2)}) collective-permute-start(f32[8,128]{1,0:T(8,128)S(1)} %max.33), channel_id=1, source_target_pairs={{0,1},{1,0},{2,3},{3,2},{4,5},{5,4},{6,7},{7,6},{8,9},{9,8},{10,11... | collective-permute-start | bytes 12296 | tf_op jit(solution)/shard_map/ppermute | solution.py:217
  83.5 2.3 %collective-permute-start.13 = (f32[8,128]{1,0:T(8,128)S(1)}, f32[8,128]{1,0:T(8,128)S(1)}, u32[]{:S(2)}, u32[]{:S(2)}) collective-permute-start(f32[8,128]{1,0:T(8,128)S(1)} %max.33), channel_id=1, source_target_pairs={{0,8},{1,9},{2,10},{3,11},{4,12},{5,13},{6,14},{7,15},{8,0},{9,1},... | collective-permute-start | bytes 12296 | tf_op jit(solution)/shard_map/ppermute | solution.py:217
  85.8 5.5 %collective-permute-start.18 = (f32[8,128]{1,0:T(8,128)S(1)}, f32[8,128]{1,0:T(8,128)S(1)}, u32[]{:S(2)}, u32[]{:S(2)}) collective-permute-start(f32[8,128]{1,0:T(8,128)S(1)} %maximum_maximum_fusion.1), channel_id=1, source_target_pairs={{0,6},{1,7},{2,4},{3,5},{4,2},{5,3},{6,0},{7,1},{8,14},{9,15},{10,... | collective-permute-start | bytes 12296 | tf_op jit(solution)/shard_map/ppermute | solution.py:217
  88.2 4.5 %collective-permute-start.17 = (f32[8,128]{1,0:T(8,128)S(1)}, f32[8,128]{1,0:T(8,128)S(1)}, u32[]{:S(2)}, u32[]{:S(2)}) collective-permute-start(f32[8,128]{1,0:T(8,128)S(1)} %maximum_maximum_fusion.1), channel_id=1, source_target_pairs={{0,4},{1,5},{2,6},{3,7},{4,0},{5,1},{6,2},{7,3},{8,12},{9,13},{10,... | collective-permute-start | bytes 12296 | tf_op jit(solution)/shard_map/ppermute | solution.py:217
  88.2 4.5 %collective-permute-start.16 = (f32[8,128]{1,0:T(8,128)S(1)}, f32[8,128]{1,0:T(8,128)S(1)}, u32[]{:S(2)}, u32[]{:S(2)}) collective-permute-start(f32[8,128]{1,0:T(8,128)S(1)} %maximum_maximum_fusion.1), channel_id=1, source_target_pairs={{0,2},{1,3},{2,0},{3,1},{4,6},{5,7},{6,4},{7,5},{8,10},{9,11},{10,... | collective-permute-start | bytes 12296 | tf_op jit(solution)/shard_map/ppermute | solution.py:217

commit v2 on v1

--- a/solution.py
+++ b/solution.py
@@ -10,7 +10,7 @@
 
 clip_ratio = 0.5
 format_limit = 448.0
-EIGHTHS = (1, 2, 2, 3)
+EIGHTHS = (1, 2, 3, 2)
 GROUPS = ((0, 1), (2, 3))
 
 
@@ -222,6 +222,8 @@
     def stage(value, at):
         return across(value, tuple((0, 1 << orders[r][at]) for r in range(2)))
 
+    weight = pltpu.with_memory_space_constraint(down_weight, pltpu.HBM)
+    own_acts = pltpu.with_memory_space_constraint(hidden_acts, pltpu.HBM)
     other_acts = across(hidden_acts, both(1, 0))
     peak = jnp.max(jnp.abs(hidden_acts), axis=1).astype(jnp.float32)
     for bit in range(bits):
@@ -230,7 +232,7 @@
     other_scale = across(own_scale, both(1, 0))
 
     made = products(
-        hidden_acts, other_acts, own_scale[:, None], other_scale[:, None], down_weight, cols
+        own_acts, other_acts, own_scale[:, None], other_scale[:, None], weight, cols
     )
     totals = []
     for keep, send in made:

time: 94.8 us -> 80.2 us (0.85)
  local copies, waits for them, and re-layouts: 19.7 us -> 0.99 us
  waiting for transfers between devices: 26.4 us -> 31.1 us
    unnamed x10 -> x4, local copies, waits for them, and re-layouts: 18.7 us -> 0.01 us
    ppermute x19, waiting for transfers between devices: 26.4 us -> 31.1 us  [across(): return lax.ppermute(value, ('row', 'col'), pairs)]
    pallas_call x1, Pallas kernels: 3.13 us -> 2.14 us  [products(): pl.pallas_call(last_body, out_shape=pair(widths[at]), in_specs=[VMEM, VME...]
  transfers between devices with their start and end apart: 19 -> 19, of which waited for: 12 -> 12; matrix products, arithmetic and copies ran while one was open for 3% -> 4% of each run, Pallas kernels for 11% -> 12%
where the time goes in v2:
time: 80.2 us; the launch traced here: 80 us
  waiting for transfers between devices  31.1 us (39%)
  starting transfers between devices  28.1 us (35%)
  Pallas kernels  15.2 us (19%)
  other arithmetic  3.72 us (5%)
  local copies, waits for them, and re-layouts  0.99 us (1%)
  between operations  0.82 us (1%)
    ppermute x19, waiting for transfers between devices, across(): return lax.ppermute(value, ('row', 'col'), pairs)  31.1 us
    ppermute x19, starting transfers between devices, across(): return lax.ppermute(value, ('row', 'col'), pairs)  28.1 us
    pallas_call x2, Pallas kernels, products(): pl.pallas_call(functools.partial(middle_body, begin), out_shape=(*pair(wi...  7.06 us
    pallas_call x1, Pallas kernels, products(): pl.pallas_call(functools.partial(first_body, cols), out_shape=(jax.ShapeD...  4.49 us
    pallas_call x1, Pallas kernels, products(): pl.pallas_call(last_body, out_shape=pair(widths[at]), in_specs=[VMEM, VME...  2.14 us
  transfers between devices with their start and end apart: 19, of which 12 were waited for; matrix products, arithmetic and copies ran while one was open for 4% of the time, Pallas kernels for 12%

profile of v2, /device:TPU:0, one launch (start us, length us, event | category | flops | bytes accessed | tf_op | source)
XLA Modules:
  0.0 80.0 jit_solution(10485294698721809126)
XLA Ops:
  1.2 1.4 %abs_reduce_fusion = bf16[128]{0:T(256)(128)(2,1)S(1)} fusion(bf16[128,3328]{1,0:T(8,128)(2,1)} %own_hbm.1), kind=kLoop, calls=%fused_computation.2 | loop fusion | flops 851840 | bytes 852224 | tf_op jit(solution)/shard_map/reduce_max | solution.py:228
  2.6 2.6 %collective-permute-start.1 = (f32[128]{0:T(128)S(1)}, f32[128]{0:T(128)S(1)}, u32[]{:S(2)}, u32[]{:S(2)}) collective-permute-start(f32[128]{0:T(128)S(1)} %convert_element_type.25), channel_id=1, source_target_pairs={{0,1},{1,0},{2,3},{3,2},{4,5},{5,4},{6,7},{7,6},{8,9},{9,8},{10,11... | collective-permute-start | bytes 1544 | tf_op jit(solution)/shard_map/ppermute | solution.py:217
  5.2 1.5 %collective-permute-done.1 = f32[128]{0:T(128)S(1)} collective-permute-done((f32[128]{0:T(128)S(1)}, f32[128]{0:T(128)S(1)}, u32[]{:S(2)}, u32[]{:S(2)}) %collective-permute-start.1) | collective-permute-done | bytes 544 | tf_op jit(solution)/shard_map/ppermute | solution.py:217
  6.7 2.1 %collective-permute-start.2 = (f32[128]{0:T(128)S(1)}, f32[128]{0:T(128)S(1)}, u32[]{:S(2)}, u32[]{:S(2)}) collective-permute-start(f32[128]{0:T(128)S(1)} %convert_maximum_fusion), channel_id=1, source_target_pairs={{0,2},{1,3},{2,0},{3,1},{4,6},{5,7},{6,4},{7,5},{8,10},{9,11},{10,... | collective-permute-start | bytes 1544 | tf_op jit(solution)/shard_map/ppermute | solution.py:217
  8.8 1.5 %collective-permute-done.2 = f32[128]{0:T(128)S(1)} collective-permute-done((f32[128]{0:T(128)S(1)}, f32[128]{0:T(128)S(1)}, u32[]{:S(2)}, u32[]{:S(2)}) %collective-permute-start.2) | collective-permute-done | bytes 544 | tf_op jit(solution)/shard_map/ppermute | solution.py:217
  10.3 3.0 %collective-permute-start.3 = (f32[128]{0:T(128)S(1)}, f32[128]{0:T(128)S(1)}, u32[]{:S(2)}, u32[]{:S(2)}) collective-permute-start(f32[128]{0:T(128)S(1)} %max.31), channel_id=1, source_target_pairs={{0,4},{1,5},{2,6},{3,7},{4,0},{5,1},{6,2},{7,3},{8,12},{9,13},{10,... | collective-permute-start | bytes 1544 | tf_op jit(solution)/shard_map/ppermute | solution.py:217
  13.4 1.5 %collective-permute-done.3 = f32[128]{0:T(128)S(1)} collective-permute-done((f32[128]{0:T(128)S(1)}, f32[128]{0:T(128)S(1)}, u32[]{:S(2)}, u32[]{:S(2)}) %collective-permute-start.3) | collective-permute-done | bytes 544 | tf_op jit(solution)/shard_map/ppermute | solution.py:217
  16.2 4.5 %first.1 = (bf16[256,3328]{1,0:T(8,128)(2,1)S(1)}, f32[128,512]{1,0:T(8,128)S(1)}, bf16[128,512]{1,0:T(8,128)(2,1)S(1)}, bf16[3328,1024]{1,0:T(8,128)(2,1)S(1)}) custom-call(bf16[128,3328]{1,0:T(8,128)(2,1)} %own_hbm.1, bf16[128,3328]{1,0:T(8,128)(2,1)S(1)} %collective-permute-done.other_ref, f32[128,1]{1,0:T(8,128)S(1)} %copy.6.own_scale, ...), custom_call_target="tpu_custom_call" | custom-call | flops 872415232 | bytes 3407872 | tf_op jit(solution)/shard_map/first/pallas_call | solution.py:140
  20.7 1.9 %collective-permute-start.5 = (bf16[128,512]{1,0:T(8,128)(2,1)S(1)}, bf16[128,512]{1,0:T(8,128)(2,1)S(1)}, u32[]{:S(2)}, u32[]{:S(2)}) collective-permute-start(bf16[128,512]{1,0:T(8,128)(2,1)S(1)} %get-tuple-element.20), channel_id=1, source_target_pairs={{0,1},{1,0},{2,3},{3,2},{4,5},{5,4},{6,7},{7,6},{8,10},{9,11},{10,... | collective-permute-start | bytes 393224 | tf_op jit(solution)/shard_map/ppermute | solution.py:217
  22.6 3.9 %middle.2 = (f32[128,1024]{1,0:T(8,128)S(1)}, bf16[128,1024]{1,0:T(8,128)(2,1)S(1)}, bf16[3328,1536]{1,0:T(8,128)(2,1)S(1)}) custom-call(bf16[256,3328]{1,0:T(8,128)(2,1)S(1)} %get-tuple-element.21.lhs_ref, bf16[3328,1024]{1,0:T(8,128)(2,1)S(1)} %get-tuple-element.22.weight_ref, bf16[3328,4096]{1,0:T(8,128)(2,1)} %weight_hbm.5), custom_call_target="tpu_custom_call" | custom-call | flops 1744830464 | bytes 6815744 | tf_op jit(solution)/shard_map/middle/pallas_call | solution.py:163
  26.6 3.2 %middle.3 = (f32[128,1536]{1,0:T(8,128)S(1)}, bf16[128,1536]{1,0:T(8,128)(2,1)S(1)}, bf16[3328,1024]{1,0:T(8,128)(2,1)S(1)}) custom-call(bf16[256,3328]{1,0:T(8,128)(2,1)S(1)} %get-tuple-element.21.lhs_ref, bf16[3328,1536]{1,0:T(8,128)(2,1)S(1)} %get-tuple-element.26.weight_ref, bf16[3328,4096]{1,0:T(8,128)(2,1)} %weight_hbm.5), custom_call_target="tpu_custom_call" | custom-call | flops 2617245696 | bytes 10223616 | tf_op jit(solution)/shard_map/middle/pallas_call | solution.py:163
  29.7 2.1 %last.1 = (f32[128,1024]{1,0:T(8,128)S(1)}, bf16[128,1024]{1,0:T(8,128)(2,1)S(1)}) custom-call(bf16[256,3328]{1,0:T(8,128)(2,1)S(1)} %get-tuple-element.21.lhs_ref, bf16[3328,1024]{1,0:T(8,128)(2,1)S(1)} %get-tuple-element.29.weight_ref), custom_call_target="tpu_custom_call" | custom-call | flops 1744830464 | bytes 6815744 | tf_op jit(solution)/shard_map/last/pallas_call | solution.py:174
  32.1 1.9 %collective-permute-start.6 = (bf16[128,1024]{1,0:T(8,128)(2,1)S(1)}, bf16[128,1024]{1,0:T(8,128)(2,1)S(1)}, u32[]{:S(2)}, u32[]{:S(2)}) collective-permute-start(bf16[128,1024]{1,0:T(8,128)(2,1)S(1)} %get-tuple-element.24), channel_id=1, source_target_pairs={{0,1},{1,0},{2,3},{3,2},{4,5},{5,4},{6,7},{7,6},{8,10},{9,11},{10,... | collective-permute-start | bytes 786440 | tf_op jit(solution)/shard_map/ppermute | solution.py:217
  34.3 4.0 %collective-permute-done.10 = bf16[128,1024]{1,0:T(8,128)(2,1)S(1)} collective-permute-done((bf16[128,1024]{1,0:T(8,128)(2,1)S(1)}, bf16[128,1024]{1,0:T(8,128)(2,1)S(1)}, u32[]{:S(2)}, u32[]{:S(2)}) %collective-permute-start.10) | collective-permute-done | bytes 262176 | tf_op jit(solution)/shard_map/ppermute | solution.py:217
  38.4 7.0 %collective-permute-done.9 = bf16[128,1536]{1,0:T(8,128)(2,1)S(1)} collective-permute-done((bf16[128,1536]{1,0:T(8,128)(2,1)S(1)}, bf16[128,1536]{1,0:T(8,128)(2,1)S(1)}, u32[]{:S(2)}, u32[]{:S(2)}) %collective-permute-start.9) | collective-permute-done | bytes 393248 | tf_op jit(solution)/shard_map/ppermute | solution.py:217
  45.5 1.6 %collective-permute-start.11 = (bf16[64,2560]{1,0:T(8,128)(2,1)S(1)}, bf16[64,2560]{1,0:T(8,128)(2,1)S(1)}, u32[]{:S(2)}, u32[]{:S(2)}) collective-permute-start(bf16[64,2560]{1,0:T(8,128)(2,1)S(1)} %fusion.2), channel_id=1, source_target_pairs={{0,2},{1,3},{2,0},{3,1},{4,6},{5,7},{6,4},{7,5},{8,9},{9,8},{10,11... | collective-permute-start | bytes 983048 | tf_op jit(solution)/shard_map/ppermute | solution.py:217
  47.7 4.9 %collective-permute-done.11 = bf16[64,2560]{1,0:T(8,128)(2,1)S(1)} collective-permute-done((bf16[64,2560]{1,0:T(8,128)(2,1)S(1)}, bf16[64,2560]{1,0:T(8,128)(2,1)S(1)}, u32[]{:S(2)}, u32[]{:S(2)}) %collective-permute-start.11) | collective-permute-done | bytes 327712 | tf_op jit(solution)/shard_map/ppermute | solution.py:217
  52.7 3.0 %collective-permute-start.12 = (bf16[32,2560]{1,0:T(8,128)(2,1)S(1)}, bf16[32,2560]{1,0:T(8,128)(2,1)S(1)}, u32[]{:S(2)}, u32[]{:S(2)}) collective-permute-start(bf16[32,2560]{1,0:T(8,128)(2,1)S(1)} %slice.70), channel_id=1, source_target_pairs={{0,4},{1,5},{2,6},{3,7},{4,0},{5,1},{6,2},{7,3},{8,12},{9,13},{10,... | collective-permute-start | bytes 491528 | tf_op jit(solution)/shard_map/ppermute | solution.py:217
  55.7 4.1 %collective-permute-start.8 = (bf16[32,1536]{1,0:T(8,128)(2,1)S(1)}, bf16[32,1536]{1,0:T(8,128)(2,1)S(1)}, u32[]{:S(2)}, u32[]{:S(2)}) collective-permute-start(bf16[32,1536]{1,0:T(8,128)(2,1)S(1)} %slice.71), channel_id=1, source_target_pairs={{0,4},{1,5},{2,6},{3,7},{4,0},{5,1},{6,2},{7,3},{8,12},{9,13},{10,... | collective-permute-start | bytes 294920 | tf_op jit(solution)/shard_map/ppermute | solution.py:217
  60.0 5.6 %collective-permute-done.8.got_ref = bf16[32,1536]{1,0:T(8,128)(2,1)S(1)} collective-permute-done((bf16[32,1536]{1,0:T(8,128)(2,1)S(1)}, bf16[32,1536]{1,0:T(8,128)(2,1)S(1)}, u32[]{:S(2)}, u32[]{:S(2)}) %collective-permute-start.8) | collective-permute-done | bytes 98336 | tf_op jit(solution)/shard_map/ppermute | solution.py:217
  71.4 2.3 %collective-permute-start.18 = (f32[8,128]{1,0:T(8,128)S(1)}, f32[8,128]{1,0:T(8,128)S(1)}, u32[]{:S(2)}, u32[]{:S(2)}) collective-permute-start(f32[8,128]{1,0:T(8,128)S(1)} %maximum_maximum_fusion.1), channel_id=1, source_target_pairs={{0,6},{1,7},{2,4},{3,5},{4,2},{5,3},{6,0},{7,1},{8,14},{9,15},{10,... | collective-permute-start | bytes 12296 | tf_op jit(solution)/shard_map/ppermute | solution.py:217
  73.7 2.1 %collective-permute-start.16 = (f32[8,128]{1,0:T(8,128)S(1)}, f32[8,128]{1,0:T(8,128)S(1)}, u32[]{:S(2)}, u32[]{:S(2)}) collective-permute-start(f32[8,128]{1,0:T(8,128)S(1)} %maximum_maximum_fusion.1), channel_id=1, source_target_pairs={{0,2},{1,3},{2,0},{3,1},{4,6},{5,7},{6,4},{7,5},{8,10},{9,11},{10,... | collective-permute-start | bytes 12296 | tf_op jit(solution)/shard_map/ppermute | solution.py:217
  76.9 1.4 %collective-permute-done.17 = f32[8,128]{1,0:T(8,128)S(1)} collective-permute-done((f32[8,128]{1,0:T(8,128)S(1)}, f32[8,128]{1,0:T(8,128)S(1)}, u32[]{:S(2)}, u32[]{:S(2)}) %collective-permute-start.17) | collective-permute-done | bytes 4128 | tf_op jit(solution)/shard_map/ppermute | solution.py:217
  78.8 1.2 %pad_maximum_fusion.3 = f32[4]{0:T(128)} fusion(f32[3]{0:T(128)S(1)} %bitcast.6, f32[1]{0:T(128)} %bitcast.3), kind=kLoop, calls=%fused_computation.23 | loop fusion | flops 4 | bytes 32 | tf_op jit(solution)/shard_map/concatenate | solution.py:274
  (52 shorter events, 10.7 us)
Async XLA Ops:
  0.6 15.6 %collective-permute-start = (bf16[128,3328]{1,0:T(8,128)(2,1)}, bf16[128,3328]{1,0:T(8,128)(2,1)S(1)}, u32[]{:S(2)}, u32[]{:S(2)}) collective-permute-start(bf16[128,3328]{1,0:T(8,128)(2,1)} %own_hbm.1), channel_id=1, source_target_pairs={{0,8},{1,9},{2,10},{3,11},{4,12},{5,13},{6,14},{7,15},{8,0},{9,1},... | collective-permute-start | bytes 2555912 | tf_op jit(solution)/shard_map/ppermute | solution.py:217
  2.6 4.1 %collective-permute-start.1 = (f32[128]{0:T(128)S(1)}, f32[128]{0:T(128)S(1)}, u32[]{:S(2)}, u32[]{:S(2)}) collective-permute-start(f32[128]{0:T(128)S(1)} %convert_element_type.25), channel_id=1, source_target_pairs={{0,1},{1,0},{2,3},{3,2},{4,5},{5,4},{6,7},{7,6},{8,9},{9,8},{10,11... | collective-permute-start | bytes 1544 | tf_op jit(solution)/shard_map/ppermute | solution.py:217
  6.7 3.6 %collective-permute-start.2 = (f32[128]{0:T(128)S(1)}, f32[128]{0:T(128)S(1)}, u32[]{:S(2)}, u32[]{:S(2)}) collective-permute-start(f32[128]{0:T(128)S(1)} %convert_maximum_fusion), channel_id=1, source_target_pairs={{0,2},{1,3},{2,0},{3,1},{4,6},{5,7},{6,4},{7,5},{8,10},{9,11},{10,... | collective-permute-start | bytes 1544 | tf_op jit(solution)/shard_map/ppermute | solution.py:217
  10.3 4.6 %collective-permute-start.3 = (f32[128]{0:T(128)S(1)}, f32[128]{0:T(128)S(1)}, u32[]{:S(2)}, u32[]{:S(2)}) collective-permute-start(f32[128]{0:T(128)S(1)} %max.31), channel_id=1, source_target_pairs={{0,4},{1,5},{2,6},{3,7},{4,0},{5,1},{6,2},{7,3},{8,12},{9,13},{10,... | collective-permute-start | bytes 1544 | tf_op jit(solution)/shard_map/ppermute | solution.py:217
  14.9 17.2 %copy-start.1 = (f32[128]{0:T(128)}, f32[128]{0:T(128)S(1)}, u32[]{:S(2)}) copy-start(f32[128]{0:T(128)S(1)} %add_multiply_fusion) | copy-start | bytes 1540
  14.9 1.2 %collective-permute-start.4 = (f32[128]{0:T(128)S(1)}, f32[128]{0:T(128)S(1)}, u32[]{:S(2)}, u32[]{:S(2)}) collective-permute-start(f32[128]{0:T(128)S(1)} %add_multiply_fusion), channel_id=1, source_target_pairs={{0,8},{1,9},{2,10},{3,11},{4,12},{5,13},{6,14},{7,15},{8,0},{9,1},... | collective-permute-start | bytes 1544 | tf_op jit(solution)/shard_map/ppermute | solution.py:217
  20.7 13.5 %collective-permute-start.5 = (bf16[128,512]{1,0:T(8,128)(2,1)S(1)}, bf16[128,512]{1,0:T(8,128)(2,1)S(1)}, u32[]{:S(2)}, u32[]{:S(2)}) collective-permute-start(bf16[128,512]{1,0:T(8,128)(2,1)S(1)} %get-tuple-element.20), channel_id=1, source_target_pairs={{0,1},{1,0},{2,3},{3,2},{4,5},{5,4},{6,7},{7,6},{8,10},{9,11},{10,... | collective-permute-start | bytes 393224 | tf_op jit(solution)/shard_map/ppermute | solution.py:217
  31.9 33.8 %copy-start = (f32[4]{0:T(128)S(1)}, f32[4]{0:T(128)}, u32[]{:S(2)}) copy-start(f32[4]{0:T(128)} %history.3) | copy-start | bytes 52
  31.9 6.4 %collective-permute-start.10 = (bf16[128,1024]{1,0:T(8,128)(2,1)S(1)}, bf16[128,1024]{1,0:T(8,128)(2,1)S(1)}, u32[]{:S(2)}, u32[]{:S(2)}) collective-permute-start(bf16[128,1024]{1,0:T(8,128)(2,1)S(1)} %get-tuple-element.31), channel_id=1, source_target_pairs={{0,1},{1,0},{2,3},{3,2},{4,5},{5,4},{6,7},{7,6},{8,10},{9,11},{10,... | collective-permute-start | bytes 786440 | tf_op jit(solution)/shard_map/ppermute | solution.py:217
  32.1 15.0 %collective-permute-start.6 = (bf16[128,1024]{1,0:T(8,128)(2,1)S(1)}, bf16[128,1024]{1,0:T(8,128)(2,1)S(1)}, u32[]{:S(2)}, u32[]{:S(2)}) collective-permute-start(bf16[128,1024]{1,0:T(8,128)(2,1)S(1)} %get-tuple-element.24), channel_id=1, source_target_pairs={{0,1},{1,0},{2,3},{3,2},{4,5},{5,4},{6,7},{7,6},{8,10},{9,11},{10,... | collective-permute-start | bytes 786440 | tf_op jit(solution)/shard_map/ppermute | solution.py:217
  34.0 11.3 %collective-permute-start.9 = (bf16[128,1536]{1,0:T(8,128)(2,1)S(1)}, bf16[128,1536]{1,0:T(8,128)(2,1)S(1)}, u32[]{:S(2)}, u32[]{:S(2)}) collective-permute-start(bf16[128,1536]{1,0:T(8,128)(2,1)S(1)} %get-tuple-element.28), channel_id=1, source_target_pairs={{0,1},{1,0},{2,3},{3,2},{4,5},{5,4},{6,7},{7,6},{8,10},{9,11},{10,... | collective-permute-start | bytes 1179656 | tf_op jit(solution)/shard_map/ppermute | solution.py:217
  45.5 7.1 %collective-permute-start.11 = (bf16[64,2560]{1,0:T(8,128)(2,1)S(1)}, bf16[64,2560]{1,0:T(8,128)(2,1)S(1)}, u32[]{:S(2)}, u32[]{:S(2)}) collective-permute-start(bf16[64,2560]{1,0:T(8,128)(2,1)S(1)} %fusion.2), channel_id=1, source_target_pairs={{0,2},{1,3},{2,0},{3,1},{4,6},{5,7},{6,4},{7,5},{8,9},{9,8},{10,11... | collective-permute-start | bytes 983048 | tf_op jit(solution)/shard_map/ppermute | solution.py:217
  47.2 8.4 %collective-permute-start.7 = (bf16[64,1536]{1,0:T(8,128)(2,1)S(1)}, bf16[64,1536]{1,0:T(8,128)(2,1)S(1)}, u32[]{:S(2)}, u32[]{:S(2)}) collective-permute-start(bf16[64,1536]{1,0:T(8,128)(2,1)S(1)} %fusion.5), channel_id=1, source_target_pairs={{0,2},{1,3},{2,0},{3,1},{4,6},{5,7},{6,4},{7,5},{8,9},{9,8},{10,11... | collective-permute-start | bytes 589832 | tf_op jit(solution)/shard_map/ppermute | solution.py:217
  52.7 13.7 %collective-permute-start.12 = (bf16[32,2560]{1,0:T(8,128)(2,1)S(1)}, bf16[32,2560]{1,0:T(8,128)(2,1)S(1)}, u32[]{:S(2)}, u32[]{:S(2)}) collective-permute-start(bf16[32,2560]{1,0:T(8,128)(2,1)S(1)} %slice.70), channel_id=1, source_target_pairs={{0,4},{1,5},{2,6},{3,7},{4,0},{5,1},{6,2},{7,3},{8,12},{9,13},{10,... | collective-permute-start | bytes 491528 | tf_op jit(solution)/shard_map/ppermute | solution.py:217
  55.7 9.9 %collective-permute-start.8 = (bf16[32,1536]{1,0:T(8,128)(2,1)S(1)}, bf16[32,1536]{1,0:T(8,128)(2,1)S(1)}, u32[]{:S(2)}, u32[]{:S(2)}) collective-permute-start(bf16[32,1536]{1,0:T(8,128)(2,1)S(1)} %slice.71), channel_id=1, source_target_pairs={{0,4},{1,5},{2,6},{3,7},{4,0},{5,1},{6,2},{7,3},{8,12},{9,13},{10,... | collective-permute-start | bytes 294920 | tf_op jit(solution)/shard_map/ppermute | solution.py:217
  67.2 3.1 %collective-permute-start.15 = (f32[8,128]{1,0:T(8,128)S(1)}, f32[8,128]{1,0:T(8,128)S(1)}, u32[]{:S(2)}, u32[]{:S(2)}) collective-permute-start(f32[8,128]{1,0:T(8,128)S(1)} %max.33), channel_id=1, source_target_pairs={{0,9},{1,8},{2,11},{3,10},{4,13},{5,12},{6,15},{7,14},{8,1},{9,0},... | collective-permute-start | bytes 12296 | tf_op jit(solution)/shard_map/ppermute | solution.py:217
  67.8 3.6 %collective-permute-start.14 = (f32[8,128]{1,0:T(8,128)S(1)}, f32[8,128]{1,0:T(8,128)S(1)}, u32[]{:S(2)}, u32[]{:S(2)}) collective-permute-start(f32[8,128]{1,0:T(8,128)S(1)} %max.33), channel_id=1, source_target_pairs={{0,1},{1,0},{2,3},{3,2},{4,5},{5,4},{6,7},{7,6},{8,9},{9,8},{10,11... | collective-permute-start | bytes 12296 | tf_op jit(solution)/shard_map/ppermute | solution.py:217
  68.9 2.5 %collective-permute-start.13 = (f32[8,128]{1,0:T(8,128)S(1)}, f32[8,128]{1,0:T(8,128)S(1)}, u32[]{:S(2)}, u32[]{:S(2)}) collective-permute-start(f32[8,128]{1,0:T(8,128)S(1)} %max.33), channel_id=1, source_target_pairs={{0,8},{1,9},{2,10},{3,11},{4,12},{5,13},{6,14},{7,15},{8,0},{9,1},... | collective-permute-start | bytes 12296 | tf_op jit(solution)/shard_map/ppermute | solution.py:217
  71.4 5.5 %collective-permute-start.18 = (f32[8,128]{1,0:T(8,128)S(1)}, f32[8,128]{1,0:T(8,128)S(1)}, u32[]{:S(2)}, u32[]{:S(2)}) collective-permute-start(f32[8,128]{1,0:T(8,128)S(1)} %maximum_maximum_fusion.1), channel_id=1, source_target_pairs={{0,6},{1,7},{2,4},{3,5},{4,2},{5,3},{6,0},{7,1},{8,14},{9,15},{10,... | collective-permute-start | bytes 12296 | tf_op jit(solution)/shard_map/ppermute | solution.py:217
  73.7 4.5 %collective-permute-start.17 = (f32[8,128]{1,0:T(8,128)S(1)}, f32[8,128]{1,0:T(8,128)S(1)}, u32[]{:S(2)}, u32[]{:S(2)}) collective-permute-start(f32[8,128]{1,0:T(8,128)S(1)} %maximum_maximum_fusion.1), channel_id=1, source_target_pairs={{0,4},{1,5},{2,6},{3,7},{4,0},{5,1},{6,2},{7,3},{8,12},{9,13},{10,... | collective-permute-start | bytes 12296 | tf_op jit(solution)/shard_map/ppermute | solution.py:217
  73.7 4.5 %collective-permute-start.16 = (f32[8,128]{1,0:T(8,128)S(1)}, f32[8,128]{1,0:T(8,128)S(1)}, u32[]{:S(2)}, u32[]{:S(2)}) collective-permute-start(f32[8,128]{1,0:T(8,128)S(1)} %maximum_maximum_fusion.1), channel_id=1, source_target_pairs={{0,2},{1,3},{2,0},{3,1},{4,6},{5,7},{6,4},{7,5},{8,10},{9,11},{10,... | collective-permute-start | bytes 12296 | tf_op jit(solution)/shard_map/ppermute | solution.py:217
